TPU v7x, 256 devices: a whole 4x4x8 slice. The times are simulated.
256 devices in a mesh: depth: 32 (over y, x, core), rows: 8 (over z).
Axes of the slice: x: 4, y: 4, z: 8, core: 2. Of those that a mesh axis runs over, the one named last changes fastest.
Arguments:
- initial: float32 [32, 256, 128], P('rows'), may hold values from -6 to 6
- forward_guess: float32 [64, 32, 256, 128], P('depth', 'rows'), may hold values from -6 to 6
- adjoint_guess: float32 [64, 32, 256, 128], P('depth', 'rows'), may hold values from -6 to 6
- cotangent: float32 [32, 256, 128], P('rows'), may hold values from -6 to 6
- kernel: bfloat16 [3, 3, 128, 128], replicated, may hold values from -0.125 to 0.125
- conv_bias: float32 [128], replicated, may hold values from -1.5 to 1.5
Outputs:
- states: float32 [64, 32, 256, 128], P('depth', 'rows')
- adjoints: float32 [64, 32, 256, 128], P('depth', 'rows')
- grad_kernel: float32 [3, 3, 128, 128], replicated
- grad_bias: float32 [128], replicated
All inputs are finite; a program needn't handle non-finite values.
Results may differ from a plain program's by a relative error of at most 0.0025.
The roundings to bfloat16 on the way count: a program that leaves them out, or rounds other values in their place, can miss the bound.
Values may be sent and summed in bfloat16 or wider, within the bound.
No kernel may reach another device: no remote copies, remote signals or barrier semaphores. Data moves between devices by JAX's collectives and lax.ppermute only.
A program may use at most 64 MiB of HBM per device.

v0:
```python
import jax
import jax.numpy as jnp
from jax import lax
from jax.sharding import PartitionSpec as P

STEP_SIZE = 0.2


def padded_2(shard, sides, width):
    for axis, dim in sides:
        devices, length = (lax.axis_size(axis), shard.shape[dim])
        up = [(i, (i + 1) % devices) for i in range(devices - 1)]
        down = [(j, i) for i, j in up]
        last = lax.slice_in_dim(shard, length - width, length, axis=dim)
        leading = lax.slice_in_dim(shard, 0, width, axis=dim)
        before = lax.ppermute(last, axis, up)
        after = lax.ppermute(leading, axis, down)
        shard = jnp.concatenate([before, shard, after], axis=dim)
    return shard


def passed_along(value, axis, steps):
    count = lax.axis_size(axis)
    leading, last = (max(0, -steps), min(count, count - steps))
    return lax.ppermute(value, axis, [(source, source + steps) for source in range(leading, last)])


def restrict(signal):
    row_count, col_count, channels = signal.shape
    return signal.reshape(row_count // 2, 2, col_count // 2, 2, channels).mean(axis=(1, 3))


def prolong(signal):
    return jnp.repeat(jnp.repeat(signal, 2, axis=0), 2, axis=1)


def taps_product(padded, kernel, row_count, col_count):
    summed = jnp.zeros((row_count * col_count, kernel.shape[3]), jnp.float32)
    for row_tap in range(3):
        for col_tap in range(3):
            window = padded[row_tap : row_tap + row_count, col_tap : col_tap + col_count].reshape(
                row_count * col_count, -1
            )
            summed = summed + jnp.dot(
                window, kernel[row_tap, col_tap], preferred_element_type=jnp.float32
            )
    return summed.reshape(row_count, col_count, -1)


def surround(signal, on_coarse):
    if on_coarse:
        padded = padded_2(signal, (("rows", 0),), 1)
    else:
        padded = padded_2(signal, (("rows", 0),), 1)
    return jnp.pad(padded, ((0, 0), (1, 1), (0, 0)))


def advance(current, kernel, conv_bias, on_coarse):
    factor = 2.0 * STEP_SIZE if on_coarse else STEP_SIZE
    squashed = jnp.tanh(current).astype(jnp.bfloat16)
    padded = surround(squashed, on_coarse)
    return current + factor * (
        taps_product(padded, kernel, current.shape[0], current.shape[1]) + conv_bias
    )


def retreat(current, adjoint, kernel_flip, on_coarse):
    factor = 2.0 * STEP_SIZE if on_coarse else STEP_SIZE
    derivative = 1.0 - jnp.tanh(current) ** 2
    padded = surround(adjoint.astype(jnp.bfloat16), on_coarse)
    return adjoint + factor * derivative * taps_product(
        padded, kernel_flip, adjoint.shape[0], adjoint.shape[1]
    )


def kernel_terms(padded, cotan, row_count, col_count):
    flat = cotan.reshape(row_count * col_count, -1)
    tap_rows = []
    for row_tap in range(3):
        tap_cols = []
        for col_tap in range(3):
            window = padded[row_tap : row_tap + row_count, col_tap : col_tap + col_count].reshape(
                row_count * col_count, -1
            )
            tap_cols.append(
                lax.dot_general(
                    window, flat, (((0,), (0,)), ((), ())), preferred_element_type=jnp.float32
                )
            )
        tap_rows.append(jnp.stack(tap_cols))
    return jnp.stack(tap_rows)


def shards(initial, forward_guess, adjoint_guess, cotangent, kernel, conv_bias):
    block_count = lax.axis_size("depth")
    depth_pos = lax.axis_index("depth")
    at_first = depth_pos == 0
    at_last = depth_pos == block_count - 1
    row_count, col_count = (initial.shape[0], initial.shape[1])
    kernel_flip = jnp.transpose(jnp.flip(kernel, (0, 1)), (0, 1, 3, 2))
    coarse_start = restrict(initial)
    guess_point = forward_guess[1]
    previous = passed_along(guess_point, "depth", 1)
    previous = jnp.where(at_first, initial, previous)
    relaxed_odd = advance(previous, kernel, conv_bias, False)
    rhs_local = restrict(advance(relaxed_odd, kernel, conv_bias, False)) - advance(
        restrict(previous), kernel, conv_bias, True
    )

    def forward_turn(step_no, state_pair):
        incoming, kept_state = state_pair
        result = advance(incoming, kernel, conv_bias, True) + rhs_local
        kept_state = jnp.where(step_no == depth_pos, result, kept_state)
        incoming = passed_along(result, "depth", 1)
        return (incoming, kept_state)

    last_coarse, stored = lax.fori_loop(
        0, block_count, forward_turn, (coarse_start, jnp.zeros_like(coarse_start))
    )
    corrected = guess_point + prolong(stored - restrict(guess_point))
    prev_fixed, prev_coarse = passed_along((corrected, stored), "depth", 1)
    prev_fixed = jnp.where(at_first, initial, prev_fixed)
    linear = jnp.where(at_first, coarse_start, prev_coarse)
    state_odd = advance(prev_fixed, kernel, conv_bias, False)
    guess_even = adjoint_guess[0]
    ahead = passed_along(guess_even, "depth", -1)
    ahead = jnp.where(at_last, cotangent, ahead)
    relaxed_adj = retreat(state_odd, ahead, kernel_flip, False)
    residual = retreat(prev_fixed, relaxed_adj, kernel_flip, False) - guess_even
    coarse_res = restrict(residual)

    def backward_turn(step_no, state_pair):
        incoming, kept_error = state_pair
        result = retreat(linear, incoming, kernel_flip, True) + coarse_res
        kept_error = jnp.where(step_no == block_count - 1 - depth_pos, result, kept_error)
        incoming = passed_along(result, "depth", -1)
        return (incoming, kept_error)

    final_error, error_own = lax.fori_loop(
        0, block_count, backward_turn, (jnp.zeros_like(coarse_start), jnp.zeros_like(coarse_start))
    )
    corrected_adj = guess_even + prolong(error_own)
    ahead_fixed = passed_along(corrected_adj, "depth", -1)
    ahead_fixed = jnp.where(at_last, cotangent, ahead_fixed)
    adjoint_odd = retreat(state_odd, ahead_fixed, kernel_flip, False)
    squashed_even = surround(jnp.tanh(prev_fixed).astype(jnp.bfloat16), False)
    squashed_odd = surround(jnp.tanh(state_odd).astype(jnp.bfloat16), False)
    local_grad = kernel_terms(squashed_even, adjoint_odd.astype(jnp.bfloat16), row_count, col_count)
    local_grad = local_grad + kernel_terms(
        squashed_odd, ahead_fixed.astype(jnp.bfloat16), row_count, col_count
    )
    local_bias = jnp.sum(adjoint_odd, axis=(0, 1)) + jnp.sum(ahead_fixed, axis=(0, 1))
    grad_sum, bias_sum = lax.psum((local_grad, local_bias), ("depth", "rows"))
    factor = STEP_SIZE / (row_count * lax.axis_size("rows") * col_count)
    states_out = jnp.stack([state_odd, corrected])
    adjoints_out = jnp.stack([corrected_adj, adjoint_odd])
    return (states_out, adjoints_out, grad_sum * factor, bias_sum * factor)


def solution(mesh):
    placed = (
        P("rows", None, None),
        P("depth", "rows", None, None),
        P("depth", "rows", None, None),
        P("rows", None, None),
        P(),
        P(),
    )
    return jax.shard_map(
        shards,
        mesh=mesh,
        in_specs=placed,
        out_specs=(P("depth", "rows", None, None), P("depth", "rows", None, None), P(), P()),
        check_vma=False,
    )
```

profile of v0, /device:TPU:1, one launch (start us, length us, event | category | flops | bytes accessed | tf_op | source)
XLA Modules:
  0.0 1818.0 jit_solution(15526250043578704130)
XLA Ops:
  86.5 6.4 collective-permute-start.9
  127.0 579.7 %while.36 = (s32[]{:T(128)}, f32[2,128,128]{2,1,0:T(8,128)S(1)}, f32[2,128,128]{2,1,0:T(8,128)S(1)}, bf16[3,3,128,128]{3,2,1,0:T(8,128)(2,1)S(1)}, f32[128]{0:T(...) while((s32[]{:T(128)}, f32[2,128,128]{2,1,0:T(8,128)S(1)}, ...), condition=%wide.region_4.5_spmd.clone, body=%wide.region_3.4_spmd.clone.sunk | while | flops 76853248 | bytes 6327017 | solution.py:117
  135.8 6.4 collective-permute-start.2
  195.1 5.8 collective-permute-start.1
  211.9 5.8 collective-permute-start.1
  228.8 5.8 collective-permute-start.1
  245.7 5.8 collective-permute-start.1
  279.4 5.8 collective-permute-start.1
  338.3 6.1 collective-permute-start.2
  355.8 7.6 collective-permute-start.2
  374.8 7.6 collective-permute-start.2
  393.7 7.6 collective-permute-start.2
  412.7 7.6 collective-permute-start.2
  431.7 7.6 collective-permute-start.2
  450.6 7.6 collective-permute-start.2
  469.6 7.6 collective-permute-start.2
  488.5 7.6 collective-permute-start.2
  507.5 7.6 collective-permute-start.2
  526.5 7.6 collective-permute-start.2
  545.4 7.6 collective-permute-start.2
  564.4 7.6 collective-permute-start.2
  583.4 7.6 collective-permute-start.2
  602.3 7.6 collective-permute-start.2
  621.3 7.6 collective-permute-start.2
  640.3 7.6 collective-permute-start.2
  659.2 7.6 collective-permute-start.2
  678.2 7.6 collective-permute-start.2
  697.2 7.6 collective-permute-start.2
  708.0 6.6 collective-permute-start.13
  731.3 7.4 collective-permute-start.16
  765.8 6.4 collective-permute-start.20
  810.8 659.7 %while.37 = (s32[]{:T(128)}, f32[2,128,128]{2,1,0:T(8,128)S(1)}, f32[2,128,128]{2,1,0:T(8,128)S(1)}, f32[2,128,128]{2,1,0:T(8,128)S(1)}, bf16[3,3,128,128]{3,2,1...) while((s32[]{:T(128)}, f32[2,128,128]{2,1,0:T(8,128)S(1)}, ...), condition=%wide.region_8.9_spmd.clone, body=%wide.region_7.8_spmd.clone.sunk | while | flops 76886016 | bytes 7244093 | solution.py:139
  824.9 10.2 collective-permute-done.5
  848.6 6.0 collective-permute-done.5
  868.0 10.2 collective-permute-done.5
  911.1 10.8 collective-permute-done.5
  954.2 6.3 collective-permute-done.5
  974.2 6.7 collective-permute-done.5
  994.6 6.7 collective-permute-done.5
  1015.0 6.7 collective-permute-done.5
  1035.4 6.7 collective-permute-done.5
  1055.8 6.7 collective-permute-done.5
  1076.2 6.7 collective-permute-done.5
  1096.6 6.7 collective-permute-done.5
  1117.0 6.7 collective-permute-done.5
  1137.5 6.7 collective-permute-done.5
  1157.9 6.7 collective-permute-done.5
  1178.3 6.7 collective-permute-done.5
  1198.7 6.7 collective-permute-done.5
  1219.1 6.7 collective-permute-done.5
  1239.5 6.7 collective-permute-done.5
  1259.9 6.7 collective-permute-done.5
  1280.3 6.7 collective-permute-done.5
  1300.7 6.7 collective-permute-done.5
  1321.1 6.7 collective-permute-done.5
  1341.5 6.7 collective-permute-done.5
  1361.9 6.7 collective-permute-done.5
  1382.3 6.7 collective-permute-done.5
  1402.7 6.7 collective-permute-done.5
  1423.1 6.7 collective-permute-done.5
  1443.5 6.7 collective-permute-done.5
  1463.9 6.7 collective-permute-done.5
  1531.3 105.2 %psum.15 = f32[128]{0:T(128)S(1)} all-reduce(f32[128]{0:T(128)S(1)} %add.599), channel_id=1, replica_groups=mesh['depth'=32,'rows'=8] {'depth','rows'}, use_global_device_ids=true, to_apply=%region_12.13 | all-reduce | flops 128 | bytes 1024 | tf_op jit(solution)/shard_map/psum | solution.py:153
  1637.0 172.2 %all-reduce.12.cloned.1.call-done = f32[3,3,128,128]{3,2,1,0:T(8,128)} async-done(((f32[3,3,128,128]{3,2,1,0:T(8,128)}), f32[3,3,128,128]{3,2,1,0:T(8,128)}) %all-reduce.12.cloned.1.call-update) | async-done | bytes 589840 | tf_op jit(solution)/shard_map/psum | solution.py:153
  (1920 shorter events, 1093.4 us)
Async XLA Ops:
  7.2 1802.1 %all-reduce.12.cloned.1.call-start = ((), (), s32[]{:S(2)}) async-start(), calls=%async_computation | async-start | bytes 1179648 | tf_op jit(solution)/shard_map/psum | solution.py:153
  8.4 13.3 collective-permute-start.17
  27.8 16.5 collective-permute-start.11
  31.3 14.3 collective-permute-start.12
  35.0 14.3 collective-permute-start.18
  39.0 10.3 collective-permute-start.19
  40.3 19.8 %collective-permute-start.7 = (bf16[1,256,128]{1,2,0:T(8,128)(2,1)}, bf16[1,256,128]{1,2,0:T(8,128)(2,1)S(1)}, u32[]{:S(2)}, u32[]{:S(2)}) collective-permute-start(bf16[1,256,128]{1,2,0:T(8,128)(2,1)} %get-tuple-element.543), channel_id=1, source_target_pairs={{0,1},{1,2},{2,3},{3,4},{4,5},{5,6},{6,7},{8,9},{9,10},{10,11},{11... | collective-permute-start | bytes 196616 | tf_op jit(solution)/shard_map/ppermute | solution.py:16
  44.3 15.8 collective-permute-start.8
  85.2 13.3 collective-permute-start.10
  86.5 12.0 collective-permute-start.9
  355.8 9.5 collective-permute-start.2
  374.8 9.5 collective-permute-start.2
  393.7 9.5 collective-permute-start.2
  412.7 9.5 collective-permute-start.2
  431.7 9.5 collective-permute-start.2
  450.6 9.5 collective-permute-start.2
  469.6 9.5 collective-permute-start.2
  488.5 9.5 collective-permute-start.2
  507.5 9.5 collective-permute-start.2
  526.5 9.5 collective-permute-start.2
  545.4 9.5 collective-permute-start.2
  564.4 9.5 collective-permute-start.2
  583.4 9.5 collective-permute-start.2
  602.3 9.5 collective-permute-start.2
  621.3 9.5 collective-permute-start.2
  640.3 9.5 collective-permute-start.2
  659.2 9.5 collective-permute-start.2
  678.2 9.5 collective-permute-start.2
  697.2 9.5 collective-permute-start.2
  708.0 13.0 collective-permute-start.13
  723.7 16.0 collective-permute-start.14
  728.8 10.8 collective-permute-start.15
  731.3 42.4 %collective-permute-start.16 = (f32[2,128,128]{2,1,0:T(8,128)S(1)}, f32[2,128,128]{2,1,0:T(8,128)}, u32[]{:S(2)}, u32[]{:S(2)}) collective-permute-start(f32[2,128,128]{2,1,0:T(8,128)S(1)} %get-tuple-element.361), channel_id=1, source_target_pairs={{0,8},{8,16},{16,24},{24,32},{32,40},{40,48},{48,56},{56,64},{64,7... | collective-permute-start | bytes 393224 | tf_op jit(solution)/shard_map/ppermute | solution.py:25
  765.8 9.7 collective-permute-start.20
  823.0 12.2 collective-permute-start.5
  866.0 12.1 collective-permute-start.5
  909.1 12.7 collective-permute-start.5
  972.3 8.6 collective-permute-start.5
  992.7 8.6 collective-permute-start.5
  1013.1 8.6 collective-permute-start.5
  1033.5 8.6 collective-permute-start.5
  1053.9 8.6 collective-permute-start.5
  1074.3 8.6 collective-permute-start.5
  1094.7 8.6 collective-permute-start.5
  1115.1 8.6 collective-permute-start.5
  1135.5 8.6 collective-permute-start.5
  1155.9 8.6 collective-permute-start.5
  1176.3 8.6 collective-permute-start.5
  1196.7 8.6 collective-permute-start.5
  1217.1 8.6 collective-permute-start.5
  1237.6 8.6 collective-permute-start.5
  1258.0 8.6 collective-permute-start.5
  1278.4 8.6 collective-permute-start.5
  1298.8 8.6 collective-permute-start.5
  1319.2 8.6 collective-permute-start.5
  1339.6 8.6 collective-permute-start.5
  1360.0 8.6 collective-permute-start.5
  1380.4 8.6 collective-permute-start.5
  1400.8 8.6 collective-permute-start.5
  1421.2 8.6 collective-permute-start.5
  1441.6 8.6 collective-permute-start.5
  1475.5 18.2 %collective-permute-start.22 = (f32[4,256,128]{1,2,0:T(8,128)}, f32[4,256,128]{1,2,0:T(8,128)}, u32[]{:S(2)}, u32[]{:S(2)}) collective-permute-start(f32[4,256,128]{1,2,0:T(8,128)} %bitcast_add_fusion), channel_id=1, source_target_pairs={{8,0},{16,8},{24,16},{32,24},{40,32},{48,40},{56,48},{64,56},{72,6... | collective-permute-start | bytes 1572872 | tf_op jit(solution)/shard_map/ppermute | solution.py:25
  1480.7 12.7 collective-permute-start.25
  1498.4 9.9 collective-permute-start.23
  (330 other events, 1910.8 us)
Sparse Core Ops, SparseCore 0:
  1529.7 279.5 all-reduce.11
where the time goes:
time: 1830 us; the launch traced here: 1820 us
  starting transfers between devices  785 us (43%)
  waiting for transfers between devices  524 us (29%)
  local copies, waits for them, and re-layouts  184 us (10%)
  matrix products  117 us (6%)
  blocking collectives  105 us (6%)
  other arithmetic  78.5 us (4%)
    ppermute x72, starting transfers between devices, padded_2(): before = lax.ppermute(last, axis, up)  393 us
    ppermute x69, starting transfers between devices, passed_along(): lax.ppermute(value, axis, [(source, source + steps) for source in range(l...  299 us
    ppermute x69, waiting for transfers between devices, passed_along(): lax.ppermute(value, axis, [(source, source + steps) for source in range(l...  283 us
    psum x1, waiting for transfers between devices, shards(): grad_sum, bias_sum = lax.psum((local_grad, local_bias), ('depth', 'rows'))  172 us
    dot_general x639, matrix products, taps_product(): jnp.dot(window, kernel[row_tap, col_tap], preferred_element_type=jnp.floa...  113 us
    psum x1, blocking collectives, shards(): grad_sum, bias_sum = lax.psum((local_grad, local_bias), ('depth', 'rows'))  105 us
    ppermute x72, starting transfers between devices, padded_2(): after = lax.ppermute(leading, axis, down)  93.1 us
    slice x119, local copies, waits for them, and re-layouts, taps_product(): padded[row_tap:row_tap + row_count, col_tap:col_tap + col_count]  79.3 us
  transfers between devices with their start and end apart: 214, of which 132 were waited for; matrix products, arithmetic and copies ran while one was open for 4% of the time, Pallas kernels for 0%

commit v1 on v0

--- a/solution.py
+++ b/solution.py
@@ -150,7 +150,7 @@
         squashed_odd, ahead_fixed.astype(jnp.bfloat16), row_count, col_count
     )
     local_bias = jnp.sum(adjoint_odd, axis=(0, 1)) + jnp.sum(ahead_fixed, axis=(0, 1))
-    grad_sum, bias_sum = lax.psum((local_grad, local_bias), ("depth", "rows"))
+    grad_sum, bias_sum = lax.psum(lax.psum((local_grad, local_bias), "depth"), "rows")
     factor = STEP_SIZE / (row_count * lax.axis_size("rows") * col_count)
     states_out = jnp.stack([state_odd, corrected])
     adjoints_out = jnp.stack([corrected_adj, adjoint_odd])

time: 1830 us -> 1690 us (0.923)
  local copies, waits for them, and re-layouts: 184 us -> 125 us
  waiting for transfers between devices: 524 us -> 490 us
  blocking collectives: 105 us -> 76.5 us
  other arithmetic: 78.5 us -> 55.6 us
    while x192 -> x0, local copies, waits for them, and re-layouts: 36.7 us -> none
    psum x1 -> x2, waiting for transfers between devices: 172 us -> 136 us  [the longest x1 136 us: shards(): lax.psum((local_grad, local_bias), 'depth')]
    psum x1 -> x2, blocking collectives: 105 us -> 76.5 us  [the longest x1 62.4 us: shards(): lax.psum((local_grad, local_bias), 'depth')]
    select_n x32, other arithmetic: 23.5 us -> 3.13 us  [backward_turn(): jnp.where(step_no == block_count - 1 - depth_pos, result, kept_error)]
    slice x72, local copies, waits for them, and re-layouts: 24.1 us -> 4.45 us  [padded_2(): last = lax.slice_in_dim(shard, length - width, length, axis=dim)]
  transfers between devices with their start and end apart: 214 -> 215, of which waited for: 132 -> 133; matrix products, arithmetic and copies ran while one was open for 4% -> 4% of each run, Pallas kernels for 0% -> 0%
where the time goes in v1:
time: 1690 us; the launch traced here: 1670 us
  starting transfers between devices  784 us (46%)
  waiting for transfers between devices  490 us (29%)
  local copies, waits for them, and re-layouts  125 us (7%)
  matrix products  117 us (7%)
  blocking collectives  76.5 us (5%)
  other arithmetic  55.6 us (3%)
    ppermute x72, starting transfers between devices, padded_2(): before = lax.ppermute(last, axis, up)  393 us
    ppermute x69, starting transfers between devices, passed_along(): lax.ppermute(value, axis, [(source, source + steps) for source in range(l...  298 us
    ppermute x69, waiting for transfers between devices, passed_along(): lax.ppermute(value, axis, [(source, source + steps) for source in range(l...  278 us
    psum x1, waiting for transfers between devices, shards(): lax.psum((local_grad, local_bias), 'depth')  136 us
    dot_general x639, matrix products, taps_product(): jnp.dot(window, kernel[row_tap, col_tap], preferred_element_type=jnp.floa...  112 us
    ppermute x72, starting transfers between devices, padded_2(): after = lax.ppermute(leading, axis, down)  93.2 us
    slice x119, local copies, waits for them, and re-layouts, taps_product(): padded[row_tap:row_tap + row_count, col_tap:col_tap + col_count]  79.4 us
    ppermute x72, waiting for transfers between devices, padded_2(): before = lax.ppermute(last, axis, up)  63.2 us
  transfers between devices with their start and end apart: 215, of which 133 were waited for; matrix products, arithmetic and copies ran while one was open for 4% of the time, Pallas kernels for 0%

profile of v1, /device:TPU:1, one launch (start us, length us, event | category | flops | bytes accessed | tf_op | source)
XLA Modules:
  0.0 1671.5 jit_solution(5668342432423458111)
XLA Ops:
  86.5 6.4 collective-permute-start.9
  128.3 579.6 %while.36 = (s32[]{:T(128)}, f32[2,128,128]{2,1,0:T(8,128)S(1)}, f32[2,128,128]{2,1,0:T(8,128)S(1)}, bf16[3,3,128,128]{3,2,1,0:T(8,128)(2,1)S(1)}, f32[128]{0:T(...) while((s32[]{:T(128)}, f32[2,128,128]{2,1,0:T(8,128)S(1)}, ...), condition=%wide.region_4.5_spmd.clone, body=%wide.region_3.4_spmd.clone.sunk | while | flops 76853248 | bytes 6327017 | solution.py:117
  137.0 6.4 collective-permute-start.2
  196.3 5.8 collective-permute-start.1
  213.2 5.8 collective-permute-start.1
  230.1 5.8 collective-permute-start.1
  331.2 5.8 collective-permute-start.1
  339.6 6.1 collective-permute-start.2
  357.1 7.6 collective-permute-start.2
  376.0 7.6 collective-permute-start.2
  395.0 7.6 collective-permute-start.2
  414.0 7.6 collective-permute-start.2
  432.9 7.6 collective-permute-start.2
  451.9 7.6 collective-permute-start.2
  470.8 7.6 collective-permute-start.2
  489.8 7.6 collective-permute-start.2
  508.8 7.6 collective-permute-start.2
  527.7 7.6 collective-permute-start.2
  546.7 7.6 collective-permute-start.2
  565.7 7.6 collective-permute-start.2
  584.6 7.6 collective-permute-start.2
  603.6 7.6 collective-permute-start.2
  622.6 7.6 collective-permute-start.2
  641.5 7.6 collective-permute-start.2
  660.5 7.6 collective-permute-start.2
  679.5 7.6 collective-permute-start.2
  698.4 7.6 collective-permute-start.2
  709.3 6.6 collective-permute-start.13
  724.2 5.8 collective-permute-start.14
  732.5 6.4 collective-permute-start.16
  767.6 5.8 collective-permute-start.20
  810.2 578.3 %while.37 = (s32[]{:T(128)}, f32[2,128,128]{2,1,0:T(8,128)S(1)}, f32[2,128,128]{2,1,0:T(8,128)S(1)}, f32[2,128,128]{2,1,0:T(8,128)S(1)}, bf16[3,3,128,128]{3,2,1...) while((s32[]{:T(128)}, f32[2,128,128]{2,1,0:T(8,128)S(1)}, ...), condition=%wide.region_8.9_spmd.clone, body=%wide.region_7.8_spmd.clone.sunk | while | flops 76886016 | bytes 6457577 | solution.py:139
  821.9 11.0 collective-permute-done.5
  859.8 11.0 collective-permute-done.5
  898.1 11.2 collective-permute-done.5
  936.6 6.4 collective-permute-done.5
  954.3 6.5 collective-permute-done.5
  972.2 6.5 collective-permute-done.5
  990.0 6.5 collective-permute-done.5
  1007.8 6.5 collective-permute-done.5
  1025.6 6.5 collective-permute-done.5
  1043.4 6.5 collective-permute-done.5
  1061.3 6.5 collective-permute-done.5
  1079.1 6.5 collective-permute-done.5
  1096.9 6.5 collective-permute-done.5
  1114.7 6.5 collective-permute-done.5
  1132.5 6.5 collective-permute-done.5
  1150.4 6.5 collective-permute-done.5
  1168.2 6.5 collective-permute-done.5
  1186.0 6.5 collective-permute-done.5
  1203.8 6.5 collective-permute-done.5
  1221.6 6.5 collective-permute-done.5
  1239.5 6.5 collective-permute-done.5
  1257.3 6.5 collective-permute-done.5
  1275.1 6.5 collective-permute-done.5
  1292.9 6.5 collective-permute-done.5
  1310.7 6.5 collective-permute-done.5
  1328.5 6.5 collective-permute-done.5
  1346.4 6.5 collective-permute-done.5
  1364.2 6.5 collective-permute-done.5
  1382.0 6.5 collective-permute-done.5
  1441.8 136.4 %all-reduce.13.cloned.1.call-done = f32[3,3,128,128]{3,2,1,0:T(8,128)} async-done(((f32[3,3,128,128]{3,2,1,0:T(8,128)}), f32[3,3,128,128]{3,2,1,0:T(8,128)}) %all-reduce.13.cloned.1.call-update) | async-done | bytes 589840 | tf_op jit(solution)/shard_map/psum | solution.py:153
  1585.7 62.4 %psum.30 = f32[128]{0:T(128)S(1)} all-reduce(f32[128]{0:T(128)S(1)} %add.603), channel_id=1, replica_groups=mesh['depth'=32,'rows'=8] {'depth'}, use_global_device_ids=true, to_apply=%region_13.14 | all-reduce | flops 128 | bytes 1024 | tf_op jit(solution)/shard_map/psum | solution.py:153
  1648.1 14.1 psum.31
  (1732 shorter events, 1022.7 us)
Async XLA Ops:
  7.2 1571.0 %all-reduce.13.cloned.1.call-start = ((), (), s32[]{:S(2)}) async-start(), calls=%async_computation | async-start | bytes 1179648 | tf_op jit(solution)/shard_map/psum | solution.py:153
  8.4 13.3 collective-permute-start.17
  15.0 8.6 collective-permute-start.6
  27.8 16.5 collective-permute-start.11
  31.3 14.2 collective-permute-start.12
  35.0 14.3 collective-permute-start.18
  39.0 10.3 collective-permute-start.19
  40.3 20.0 %collective-permute-start.7 = (bf16[1,256,128]{1,2,0:T(8,128)(2,1)}, bf16[1,256,128]{1,2,0:T(8,128)(2,1)S(1)}, u32[]{:S(2)}, u32[]{:S(2)}) collective-permute-start(bf16[1,256,128]{1,2,0:T(8,128)(2,1)} %get-tuple-element.543), channel_id=1, source_target_pairs={{0,1},{1,2},{2,3},{3,4},{4,5},{5,6},{6,7},{8,9},{9,10},{10,11},{11... | collective-permute-start | bytes 196616 | tf_op jit(solution)/shard_map/ppermute | solution.py:16
  44.3 16.0 collective-permute-start.8
  85.2 13.3 collective-permute-start.10
  86.5 12.0 collective-permute-start.9
  357.1 9.5 collective-permute-start.2
  376.0 9.5 collective-permute-start.2
  395.0 9.5 collective-permute-start.2
  414.0 9.5 collective-permute-start.2
  432.9 9.5 collective-permute-start.2
  451.9 9.5 collective-permute-start.2
  470.8 9.5 collective-permute-start.2
  489.8 9.5 collective-permute-start.2
  508.8 9.5 collective-permute-start.2
  527.7 9.5 collective-permute-start.2
  546.7 9.5 collective-permute-start.2
  565.7 9.5 collective-permute-start.2
  584.6 9.5 collective-permute-start.2
  603.6 9.5 collective-permute-start.2
  622.6 9.5 collective-permute-start.2
  641.5 9.5 collective-permute-start.2
  660.5 9.5 collective-permute-start.2
  679.5 9.5 collective-permute-start.2
  698.4 9.5 collective-permute-start.2
  709.3 13.0 collective-permute-start.13
  724.2 15.7 collective-permute-start.14
  730.0 9.9 collective-permute-start.15
  732.5 42.3 %collective-permute-start.16 = (f32[2,128,128]{2,1,0:T(8,128)S(1)}, f32[2,128,128]{2,1,0:T(8,128)}, u32[]{:S(2)}, u32[]{:S(2)}) collective-permute-start(f32[2,128,128]{2,1,0:T(8,128)S(1)} %get-tuple-element.361), channel_id=1, source_target_pairs={{0,8},{8,16},{16,24},{24,32},{32,40},{40,48},{48,56},{56,64},{64,7... | collective-permute-start | bytes 393224 | tf_op jit(solution)/shard_map/ppermute | solution.py:25
  767.6 9.1 collective-permute-start.20
  819.9 12.9 collective-permute-start.5
  857.8 12.9 collective-permute-start.5
  896.2 13.1 collective-permute-start.5
  952.4 8.4 collective-permute-start.5
  970.2 8.4 collective-permute-start.5
  988.1 8.4 collective-permute-start.5
  1005.9 8.4 collective-permute-start.5
  1023.7 8.4 collective-permute-start.5
  1041.5 8.4 collective-permute-start.5
  1059.3 8.4 collective-permute-start.5
  1077.1 8.4 collective-permute-start.5
  1095.0 8.4 collective-permute-start.5
  1112.8 8.4 collective-permute-start.5
  1130.6 8.4 collective-permute-start.5
  1148.4 8.4 collective-permute-start.5
  1166.2 8.4 collective-permute-start.5
  1184.1 8.4 collective-permute-start.5
  1201.9 8.4 collective-permute-start.5
  1219.7 8.4 collective-permute-start.5
  1237.5 8.4 collective-permute-start.5
  1255.3 8.4 collective-permute-start.5
  1273.2 8.4 collective-permute-start.5
  1291.0 8.4 collective-permute-start.5
  1308.8 8.4 collective-permute-start.5
  1326.6 8.4 collective-permute-start.5
  1362.3 8.4 collective-permute-start.5
  1390.8 14.2 collective-permute-start.22
  1408.7 8.7 collective-permute-start.23
  1441.7 221.0 %all-reduce.15.cloned.1.call-start = ((), (), s32[]{:S(2)}) async-start(), calls=%async_computation.1 | async-start | bytes 1179648 | tf_op jit(solution)/shard_map/psum | solution.py:153
  (235 other events, 2798.9 us)
Sparse Core Ops, SparseCore 0:
  1441.8 136.3 all-reduce.12
  1580.5 69.4 all-reduce.14
